TPU v7x, 32 devices: a whole 2x2x4 slice. The times are simulated.
32 devices in a mesh: axial: 8 (over y, x, core), theta: 4 (over z).
Axes of the slice: x: 2, y: 2, z: 4, core: 2. Of those that a mesh axis runs over, the one named last changes fastest.
Arguments:
- rhs_field: float32 [16, 16, 32, 320], P('theta', 'axial'), may hold values from -6 to 6
- diag_inv: float32 [16, 16, 320, 320], P('theta', 'axial'), may hold values from -0.5 to 2
- lower_block: float32 [16, 16, 320, 320], P('theta', 'axial'), may hold values from -2 to 0.5
- upper_block: float32 [16, 16, 320, 320], P('theta', 'axial'), may hold values from -2 to 0.5
- proj_table: float32 [16, 80, 80], replicated, may hold values from -0.5 to 0.5
- intersection_list: int32 [16, 2], P('theta'), may hold values from 0 to 15
- proj_index: int32 [16, 2], P('theta'), may hold values from 0 to 15
- angle_step: int32 [1], replicated, may hold values from 0 to 15
Outputs:
- solution: float32 [16, 16, 32, 320], P('theta', 'axial')
- mortar: float32 [8, 16, 2560], P('axial', 'theta')
All inputs are finite; a program needn't handle non-finite values.
Results may differ from a plain program's by a relative error of at most 0.0002.
Values sent between devices are 32-bit elements; how exact they have to be, the bound alone decides.
No kernel may reach another device: no remote copies, remote signals or barrier semaphores. Data moves between devices by JAX's collectives and lax.ppermute only.
A program may use at most 64 MiB of HBM per device.

v0:
```python
import jax
import jax.numpy as jnp
from jax import lax
from jax.sharding import PartitionSpec as P


def shifted(value, axis, steps):
    count = lax.axis_size(axis)
    first, last = (max(0, -steps), min(count, count - steps))
    return lax.ppermute(value, axis, [(source, source + steps) for source in range(first, last)])


def product(blocks, vectors):
    return jnp.einsum("lbc,lvc->lvb", blocks, vectors, precision=lax.Precision.HIGHEST)


def forward_lines(rhs_part, inverse_part, lower_part, incoming):
    previous = incoming
    results = []
    for element in range(rhs_part.shape[1]):
        inner = rhs_part[:, element] - product(lower_part[:, element], previous)
        previous = product(inverse_part[:, element], inner)
        results.append(previous)
    return jnp.stack(results, axis=1)


def backward_lines(swept_part, inverse_part, upper_part, incoming):
    following = incoming
    results = []
    for element in reversed(range(swept_part.shape[1])):
        coupled = product(upper_part[:, element], following)
        following = swept_part[:, element] - product(inverse_part[:, element], coupled)
        results.append(following)
    return jnp.stack(results[::-1], axis=1)


def run_forward(rhs_field, diag_inv, lower_block, group_size):
    batch_total = rhs_field.shape[0] // group_size
    chain_size = lax.axis_size("axial")
    position = lax.axis_index("axial")
    boundary = jnp.zeros((group_size,) + rhs_field.shape[2:], jnp.float32)

    def advance(section_no, carried):
        result, incoming = carried
        batch_id = section_no - position
        active = jnp.logical_and(batch_id >= 0, batch_id < batch_total)
        offset = jnp.clip(batch_id, 0, batch_total - 1) * group_size

        def window(source):
            return lax.dynamic_slice_in_dim(source, offset, group_size, 0)

        def working(current):
            values = forward_lines(
                window(rhs_field), window(diag_inv), window(lower_block), incoming
            )
            return (lax.dynamic_update_slice_in_dim(current, values, offset, 0), values[:, -1])

        def waiting(current):
            return (current, boundary)

        result, edge_values = lax.cond(active, working, waiting, result)
        outgoing = shifted(edge_values, "axial", 1)
        return (result, outgoing)

    result, _ = lax.fori_loop(
        0, chain_size + batch_total - 1, advance, (jnp.zeros_like(rhs_field), boundary)
    )
    return result


def run_backward(swept, diag_inv, upper_block, group_size):
    batch_total = swept.shape[0] // group_size
    chain_size = lax.axis_size("axial")
    position = chain_size - 1 - lax.axis_index("axial")
    boundary = jnp.zeros((group_size,) + swept.shape[2:], jnp.float32)

    def advance(section_no, carried):
        result, incoming = carried
        batch_id = section_no - position
        active = jnp.logical_and(batch_id >= 0, batch_id < batch_total)
        offset = jnp.clip(batch_id, 0, batch_total - 1) * group_size

        def window(source):
            return lax.dynamic_slice_in_dim(source, offset, group_size, 0)

        def working(current):
            values = backward_lines(window(swept), window(diag_inv), window(upper_block), incoming)
            return (lax.dynamic_update_slice_in_dim(current, values, offset, 0), values[:, 0])

        def waiting(current):
            return (current, boundary)

        result, edge_values = lax.cond(active, working, waiting, result)
        outgoing = shifted(edge_values, "axial", -1)
        return (result, outgoing)

    result, _ = lax.fori_loop(
        0, chain_size + batch_total - 1, advance, (jnp.zeros_like(swept), boundary)
    )
    return result


def local(
    rhs_field,
    diag_inv,
    lower_block,
    upper_block,
    proj_table,
    intersection_list,
    proj_index,
    angle_step,
):
    lines_here = rhs_field.shape[0]
    group_size = 1
    swept = run_forward(rhs_field, diag_inv, lower_block, group_size)
    solution = run_backward(swept, diag_inv, upper_block, group_size)
    face_size = proj_table.shape[1]
    vec_count = rhs_field.shape[2]
    block_size = rhs_field.shape[3]
    intersection_count = intersection_list.shape[1]
    traces = solution[:, -1, :, block_size - face_size :].reshape(lines_here, vec_count * face_size)
    total_lines = lines_here * lax.axis_size("theta")
    sources = (intersection_list + angle_step[0]) % total_lines
    segment = lax.all_gather(traces, "theta", axis=0, tiled=True)
    row_ids = jnp.arange(segment.shape[0], dtype=jnp.int32)
    select = (sources[:, :, None] == row_ids[None, None, :]).astype(jnp.float32)
    picked = jnp.einsum("lkn,nw->lkw", select, segment, precision=lax.Precision.HIGHEST)
    one_hot = jax.nn.one_hot(proj_index, proj_table.shape[0], dtype=jnp.float32)
    chosen = jnp.einsum("gkp,pfh->gkfh", one_hot, proj_table, precision=lax.Precision.HIGHEST)
    picked = picked.reshape(lines_here, intersection_count, vec_count, face_size)
    mortar = jnp.einsum("gkfh,gkvh->gvf", chosen, picked, precision=lax.Precision.HIGHEST)
    return (solution, mortar.reshape(1, lines_here, vec_count * face_size))


def solution(mesh):
    return jax.shard_map(
        local,
        mesh=mesh,
        in_specs=(
            P("theta", "axial", None, None),
            P("theta", "axial", None, None),
            P("theta", "axial", None, None),
            P("theta", "axial", None, None),
            P(),
            P("theta", None),
            P("theta", None),
            P(),
        ),
        out_specs=(P("theta", "axial", None, None), P("axial", "theta", None)),
        check_vma=False,
    )
```

profile of v0, /device:TPU:0, one launch (start us, length us, event | category | flops | bytes accessed | tf_op | source)
XLA Modules:
  0.0 290.1 jit_solution(14650015283102837466)
XLA Ops:
  0.7 114.5 %while.36 = (s32[]{:T(128)}, f32[4,2,32,320]{3,2,1,0:T(8,128)S(1)}, f32[1,32,320]{2,1,0:T(8,128)S(1)}, s32[]{:T(128)}, f32[4,2,32,320]{3,2,1,0:T(8,128)}, /*inde...) while((s32[]{:T(128)}, f32[4,2,32,320]{3,2,1,0:T(8,128)S(1)}, ...), condition=%wide.region_3.4_spmd, body=%wide.region_0.3_spmd.sunk | while | flops 157327360 | bytes 2747687 | solution.py:65
  0.7 7.8 %conditional.4 = (f32[4,2,32,320]{3,2,1,0:T(8,128)S(1)}, f32[1,32,320]{2,1,0:T(8,128)}) conditional(s32[]{:T(128)} %convert_element_type.19, f32[4,2,32,320]{3,2,1,0:T(8,128)S(1)} %get-tuple-element.475, (s32[]{:T(128)}, f32[4,2,32,320]{3,2,1,0:T(8,128)}, f32[4,2,320,320]{3,2,1,0:T(8,128)}, f32[1,32,320]{2,1,0:T(8,128)S(1)}, ...), branch_computations={%region_1.1_spmd, %region_2.2_spmd} | conditional | flops 157327360 | bytes 2583620 | solution.py:61
  0.7 1.6 fusion
  4.0 1.6 convolution_subtract_fusion
  5.6 2.2 fusion.1
  10.9 7.8 %conditional.4 = (f32[4,2,32,320]{3,2,1,0:T(8,128)S(1)}, f32[1,32,320]{2,1,0:T(8,128)}) conditional(s32[]{:T(128)} %convert_element_type.19, f32[4,2,32,320]{3,2,1,0:T(8,128)S(1)} %get-tuple-element.475, (s32[]{:T(128)}, f32[4,2,32,320]{3,2,1,0:T(8,128)}, f32[4,2,320,320]{3,2,1,0:T(8,128)}, f32[1,32,320]{2,1,0:T(8,128)S(1)}, ...), branch_computations={%region_1.1_spmd, %region_2.2_spmd} | conditional | flops 157327360 | bytes 2583620 | solution.py:61
  14.1 1.6 convolution_subtract_fusion
  15.7 2.2 fusion.1
  18.7 2.3 collective-permute-start
  22.0 7.8 %conditional.4 = (f32[4,2,32,320]{3,2,1,0:T(8,128)S(1)}, f32[1,32,320]{2,1,0:T(8,128)}) conditional(s32[]{:T(128)} %convert_element_type.19, f32[4,2,32,320]{3,2,1,0:T(8,128)S(1)} %get-tuple-element.475, (s32[]{:T(128)}, f32[4,2,32,320]{3,2,1,0:T(8,128)}, f32[4,2,320,320]{3,2,1,0:T(8,128)}, f32[1,32,320]{2,1,0:T(8,128)S(1)}, ...), branch_computations={%region_1.1_spmd, %region_2.2_spmd} | conditional | flops 157327360 | bytes 2583620 | solution.py:61
  25.2 1.6 convolution_subtract_fusion
  26.8 2.2 fusion.1
  29.8 2.3 collective-permute-start
  33.2 7.8 %conditional.4 = (f32[4,2,32,320]{3,2,1,0:T(8,128)S(1)}, f32[1,32,320]{2,1,0:T(8,128)}) conditional(s32[]{:T(128)} %convert_element_type.19, f32[4,2,32,320]{3,2,1,0:T(8,128)S(1)} %get-tuple-element.475, (s32[]{:T(128)}, f32[4,2,32,320]{3,2,1,0:T(8,128)}, f32[4,2,320,320]{3,2,1,0:T(8,128)}, f32[1,32,320]{2,1,0:T(8,128)S(1)}, ...), branch_computations={%region_1.1_spmd, %region_2.2_spmd} | conditional | flops 157327360 | bytes 2583620 | solution.py:61
  37.9 2.2 fusion.1
  40.9 4.5 %collective-permute-start = (f32[1,32,320]{2,1,0:T(8,128)}, f32[1,32,320]{2,1,0:T(8,128)S(1)}, u32[]{:S(2)}, u32[]{:S(2)}) collective-permute-start(f32[1,32,320]{2,1,0:T(8,128)} %get-tuple-element.446), channel_id=1, source_target_pairs={{0,4},{4,8},{8,12},{12,16},{16,20},{20,24},{24,28},{1,5},{5,9},{9,... | collective-permute-start | bytes 122888 | tf_op jit(solution)/shard_map/while/body/eval_jaxpr/ppermute | solution.py:10
  47.2 11.7 %collective-permute-start = (f32[1,32,320]{2,1,0:T(8,128)}, f32[1,32,320]{2,1,0:T(8,128)S(1)}, u32[]{:S(2)}, u32[]{:S(2)}) collective-permute-start(f32[1,32,320]{2,1,0:T(8,128)} %get-tuple-element.446), channel_id=1, source_target_pairs={{0,4},{4,8},{8,12},{12,16},{16,20},{20,24},{24,28},{1,5},{5,9},{9,... | collective-permute-start | bytes 122888 | tf_op jit(solution)/shard_map/while/body/eval_jaxpr/ppermute | solution.py:10
  60.5 4.5 %collective-permute-start = (f32[1,32,320]{2,1,0:T(8,128)}, f32[1,32,320]{2,1,0:T(8,128)S(1)}, u32[]{:S(2)}, u32[]{:S(2)}) collective-permute-start(f32[1,32,320]{2,1,0:T(8,128)} %get-tuple-element.446), channel_id=1, source_target_pairs={{0,4},{4,8},{8,12},{12,16},{16,20},{20,24},{24,28},{1,5},{5,9},{9,... | collective-permute-start | bytes 122888 | tf_op jit(solution)/shard_map/while/body/eval_jaxpr/ppermute | solution.py:10
  66.8 11.7 %collective-permute-start = (f32[1,32,320]{2,1,0:T(8,128)}, f32[1,32,320]{2,1,0:T(8,128)S(1)}, u32[]{:S(2)}, u32[]{:S(2)}) collective-permute-start(f32[1,32,320]{2,1,0:T(8,128)} %get-tuple-element.446), channel_id=1, source_target_pairs={{0,4},{4,8},{8,12},{12,16},{16,20},{20,24},{24,28},{1,5},{5,9},{9,... | collective-permute-start | bytes 122888 | tf_op jit(solution)/shard_map/while/body/eval_jaxpr/ppermute | solution.py:10
  80.1 4.5 %collective-permute-start = (f32[1,32,320]{2,1,0:T(8,128)}, f32[1,32,320]{2,1,0:T(8,128)S(1)}, u32[]{:S(2)}, u32[]{:S(2)}) collective-permute-start(f32[1,32,320]{2,1,0:T(8,128)} %get-tuple-element.446), channel_id=1, source_target_pairs={{0,4},{4,8},{8,12},{12,16},{16,20},{20,24},{24,28},{1,5},{5,9},{9,... | collective-permute-start | bytes 122888 | tf_op jit(solution)/shard_map/while/body/eval_jaxpr/ppermute | solution.py:10
  86.4 6.8 %collective-permute-start = (f32[1,32,320]{2,1,0:T(8,128)}, f32[1,32,320]{2,1,0:T(8,128)S(1)}, u32[]{:S(2)}, u32[]{:S(2)}) collective-permute-start(f32[1,32,320]{2,1,0:T(8,128)} %get-tuple-element.446), channel_id=1, source_target_pairs={{0,4},{4,8},{8,12},{12,16},{16,20},{20,24},{24,28},{1,5},{5,9},{9,... | collective-permute-start | bytes 122888 | tf_op jit(solution)/shard_map/while/body/eval_jaxpr/ppermute | solution.py:10
  94.8 5.0 %collective-permute-start = (f32[1,32,320]{2,1,0:T(8,128)}, f32[1,32,320]{2,1,0:T(8,128)S(1)}, u32[]{:S(2)}, u32[]{:S(2)}) collective-permute-start(f32[1,32,320]{2,1,0:T(8,128)} %get-tuple-element.446), channel_id=1, source_target_pairs={{0,4},{4,8},{8,12},{12,16},{16,20},{20,24},{24,28},{1,5},{5,9},{9,... | collective-permute-start | bytes 122888 | tf_op jit(solution)/shard_map/while/body/eval_jaxpr/ppermute | solution.py:10
  101.5 12.6 %collective-permute-start = (f32[1,32,320]{2,1,0:T(8,128)}, f32[1,32,320]{2,1,0:T(8,128)S(1)}, u32[]{:S(2)}, u32[]{:S(2)}) collective-permute-start(f32[1,32,320]{2,1,0:T(8,128)} %get-tuple-element.446), channel_id=1, source_target_pairs={{0,4},{4,8},{8,12},{12,16},{16,20},{20,24},{24,28},{1,5},{5,9},{9,... | collective-permute-start | bytes 122888 | tf_op jit(solution)/shard_map/while/body/eval_jaxpr/ppermute | solution.py:10
  115.3 156.4 %while.37 = (s32[]{:T(128)}, f32[4,2,32,320]{3,2,1,0:T(8,128)S(1)}, f32[1,32,320]{2,1,0:T(8,128)S(1)}, s32[]{:T(128)}, f32[4,2,32,320]{3,2,1,0:T(8,128)S(1)}, /*...) while((s32[]{:T(128)}, f32[4,2,32,320]{3,2,1,0:T(8,128)S(1)}, ...), condition=%wide.region_7.8_spmd, body=%wide.region_4.7_spmd.sunk | while | flops 157327360 | bytes 2731303 | solution.py:97
  117.2 5.1 %collective-permute-done.1 = f32[1,32,320]{2,1,0:T(8,128)S(1)} collective-permute-done((f32[1,32,320]{2,1,0:T(8,128)}, f32[1,32,320]{2,1,0:T(8,128)S(1)}, u32[]{:S(2)}, u32[]{:S(2)}) %collective-permute-start.1) | collective-permute-done | bytes 40992 | tf_op jit(solution)/shard_map/while/body/eval_jaxpr/ppermute | solution.py:10
  124.2 6.1 %collective-permute-done.1 = f32[1,32,320]{2,1,0:T(8,128)S(1)} collective-permute-done((f32[1,32,320]{2,1,0:T(8,128)}, f32[1,32,320]{2,1,0:T(8,128)S(1)}, u32[]{:S(2)}, u32[]{:S(2)}) %collective-permute-start.1) | collective-permute-done | bytes 40992 | tf_op jit(solution)/shard_map/while/body/eval_jaxpr/ppermute | solution.py:10
  132.3 5.1 %collective-permute-done.1 = f32[1,32,320]{2,1,0:T(8,128)S(1)} collective-permute-done((f32[1,32,320]{2,1,0:T(8,128)}, f32[1,32,320]{2,1,0:T(8,128)S(1)}, u32[]{:S(2)}, u32[]{:S(2)}) %collective-permute-start.1) | collective-permute-done | bytes 40992 | tf_op jit(solution)/shard_map/while/body/eval_jaxpr/ppermute | solution.py:10
  139.2 8.8 %collective-permute-done.1 = f32[1,32,320]{2,1,0:T(8,128)S(1)} collective-permute-done((f32[1,32,320]{2,1,0:T(8,128)}, f32[1,32,320]{2,1,0:T(8,128)S(1)}, u32[]{:S(2)}, u32[]{:S(2)}) %collective-permute-start.1) | collective-permute-done | bytes 40992 | tf_op jit(solution)/shard_map/while/body/eval_jaxpr/ppermute | solution.py:10
  150.0 5.2 %collective-permute-done.1 = f32[1,32,320]{2,1,0:T(8,128)S(1)} collective-permute-done((f32[1,32,320]{2,1,0:T(8,128)}, f32[1,32,320]{2,1,0:T(8,128)S(1)}, u32[]{:S(2)}, u32[]{:S(2)}) %collective-permute-start.1) | collective-permute-done | bytes 40992 | tf_op jit(solution)/shard_map/while/body/eval_jaxpr/ppermute | solution.py:10
  157.1 6.0 %collective-permute-done.1 = f32[1,32,320]{2,1,0:T(8,128)S(1)} collective-permute-done((f32[1,32,320]{2,1,0:T(8,128)}, f32[1,32,320]{2,1,0:T(8,128)S(1)}, u32[]{:S(2)}, u32[]{:S(2)}) %collective-permute-start.1) | collective-permute-done | bytes 40992 | tf_op jit(solution)/shard_map/while/body/eval_jaxpr/ppermute | solution.py:10
  165.0 52.2 %collective-permute-done.1 = f32[1,32,320]{2,1,0:T(8,128)S(1)} collective-permute-done((f32[1,32,320]{2,1,0:T(8,128)}, f32[1,32,320]{2,1,0:T(8,128)S(1)}, u32[]{:S(2)}, u32[]{:S(2)}) %collective-permute-start.1) | collective-permute-done | bytes 40992 | tf_op jit(solution)/shard_map/while/body/eval_jaxpr/ppermute | solution.py:10
  217.2 7.9 %conditional.5 = (f32[4,2,32,320]{3,2,1,0:T(8,128)S(1)}, f32[1,32,320]{2,1,0:T(8,128)}) conditional(s32[]{:T(128)} %convert_element_type.20, f32[4,2,32,320]{3,2,1,0:T(8,128)S(1)} %get-tuple-element.505, (s32[]{:T(128)}, f32[4,2,32,320]{3,2,1,0:T(8,128)S(1)}, f32[4,2,320,320]{3,2,1,0:T(8,128)}, f32[1,32,320]{2,1,0:T(8,128)S(1)}, ...), branch_computations={%region_5.5_spmd, %region_6.6_spmd} | conditional | flops 157327360 | bytes 2567236 | solution.py:93
  218.8 1.7 convolution_subtract_fusion.1
  222.1 2.2 convolution_subtract_fusion.2
  226.4 5.2 %collective-permute-done.1 = f32[1,32,320]{2,1,0:T(8,128)S(1)} collective-permute-done((f32[1,32,320]{2,1,0:T(8,128)}, f32[1,32,320]{2,1,0:T(8,128)S(1)}, u32[]{:S(2)}, u32[]{:S(2)}) %collective-permute-start.1) | collective-permute-done | bytes 40992 | tf_op jit(solution)/shard_map/while/body/eval_jaxpr/ppermute | solution.py:10
  231.7 7.9 %conditional.5 = (f32[4,2,32,320]{3,2,1,0:T(8,128)S(1)}, f32[1,32,320]{2,1,0:T(8,128)}) conditional(s32[]{:T(128)} %convert_element_type.20, f32[4,2,32,320]{3,2,1,0:T(8,128)S(1)} %get-tuple-element.505, (s32[]{:T(128)}, f32[4,2,32,320]{3,2,1,0:T(8,128)S(1)}, f32[4,2,320,320]{3,2,1,0:T(8,128)}, f32[1,32,320]{2,1,0:T(8,128)S(1)}, ...), branch_computations={%region_5.5_spmd, %region_6.6_spmd} | conditional | flops 157327360 | bytes 2567236 | solution.py:93
  233.2 1.7 convolution_subtract_fusion.1
  236.5 2.2 convolution_subtract_fusion.2
  240.8 5.2 %collective-permute-done.1 = f32[1,32,320]{2,1,0:T(8,128)S(1)} collective-permute-done((f32[1,32,320]{2,1,0:T(8,128)}, f32[1,32,320]{2,1,0:T(8,128)S(1)}, u32[]{:S(2)}, u32[]{:S(2)}) %collective-permute-start.1) | collective-permute-done | bytes 40992 | tf_op jit(solution)/shard_map/while/body/eval_jaxpr/ppermute | solution.py:10
  246.1 7.9 %conditional.5 = (f32[4,2,32,320]{3,2,1,0:T(8,128)S(1)}, f32[1,32,320]{2,1,0:T(8,128)}) conditional(s32[]{:T(128)} %convert_element_type.20, f32[4,2,32,320]{3,2,1,0:T(8,128)S(1)} %get-tuple-element.505, (s32[]{:T(128)}, f32[4,2,32,320]{3,2,1,0:T(8,128)S(1)}, f32[4,2,320,320]{3,2,1,0:T(8,128)}, f32[1,32,320]{2,1,0:T(8,128)S(1)}, ...), branch_computations={%region_5.5_spmd, %region_6.6_spmd} | conditional | flops 157327360 | bytes 2567236 | solution.py:93
  247.6 1.7 convolution_subtract_fusion.1
  251.0 2.2 convolution_subtract_fusion.2
  255.3 5.2 %collective-permute-done.1 = f32[1,32,320]{2,1,0:T(8,128)S(1)} collective-permute-done((f32[1,32,320]{2,1,0:T(8,128)}, f32[1,32,320]{2,1,0:T(8,128)S(1)}, u32[]{:S(2)}, u32[]{:S(2)}) %collective-permute-start.1) | collective-permute-done | bytes 40992 | tf_op jit(solution)/shard_map/while/body/eval_jaxpr/ppermute | solution.py:10
  260.5 7.9 %conditional.5 = (f32[4,2,32,320]{3,2,1,0:T(8,128)S(1)}, f32[1,32,320]{2,1,0:T(8,128)}) conditional(s32[]{:T(128)} %convert_element_type.20, f32[4,2,32,320]{3,2,1,0:T(8,128)S(1)} %get-tuple-element.505, (s32[]{:T(128)}, f32[4,2,32,320]{3,2,1,0:T(8,128)S(1)}, f32[4,2,320,320]{3,2,1,0:T(8,128)}, f32[1,32,320]{2,1,0:T(8,128)S(1)}, ...), branch_computations={%region_5.5_spmd, %region_6.6_spmd} | conditional | flops 157327360 | bytes 2567236 | solution.py:93
  262.0 1.7 convolution_subtract_fusion.1
  265.4 2.2 convolution_subtract_fusion.2
  269.7 2.0 collective-permute-done.1
  271.9 15.2 %all-gather = f32[4,4,2560]{2,1,0:T(4,128)S(1)} all-gather(f32[1,4,2560]{2,1,0:T(4,128)S(1)} %reshape.100), channel_id=1, replica_groups=mesh['axial'=8,'theta'=4] {'theta'}, dimensions={0}, use_global_device_ids=true | all-gather | bytes 204800 | tf_op jit(solution)/shard_map/all_gather | solution.py:124
  (97 shorter events, 78.8 us)
Async XLA Ops:
  0.6 287.7 %copy-start = (f32[16,80,80]{2,1,0:T(8,128)S(1)}, f32[16,80,80]{2,1,0:T(8,128)}, u32[]{:S(2)}) copy-start(f32[16,80,80]{2,1,0:T(8,128)} %param.20) | copy-start | bytes 1228804
  8.6 2.4 collective-permute-start
  18.7 3.3 %collective-permute-start = (f32[1,32,320]{2,1,0:T(8,128)}, f32[1,32,320]{2,1,0:T(8,128)S(1)}, u32[]{:S(2)}, u32[]{:S(2)}) collective-permute-start(f32[1,32,320]{2,1,0:T(8,128)} %get-tuple-element.446), channel_id=1, source_target_pairs={{0,4},{4,8},{8,12},{12,16},{16,20},{20,24},{24,28},{1,5},{5,9},{9,... | collective-permute-start | bytes 122888 | tf_op jit(solution)/shard_map/while/body/eval_jaxpr/ppermute | solution.py:10
  29.8 3.4 %collective-permute-start = (f32[1,32,320]{2,1,0:T(8,128)}, f32[1,32,320]{2,1,0:T(8,128)S(1)}, u32[]{:S(2)}, u32[]{:S(2)}) collective-permute-start(f32[1,32,320]{2,1,0:T(8,128)} %get-tuple-element.446), channel_id=1, source_target_pairs={{0,4},{4,8},{8,12},{12,16},{16,20},{20,24},{24,28},{1,5},{5,9},{9,... | collective-permute-start | bytes 122888 | tf_op jit(solution)/shard_map/while/body/eval_jaxpr/ppermute | solution.py:10
  40.9 5.6 %collective-permute-start = (f32[1,32,320]{2,1,0:T(8,128)}, f32[1,32,320]{2,1,0:T(8,128)S(1)}, u32[]{:S(2)}, u32[]{:S(2)}) collective-permute-start(f32[1,32,320]{2,1,0:T(8,128)} %get-tuple-element.446), channel_id=1, source_target_pairs={{0,4},{4,8},{8,12},{12,16},{16,20},{20,24},{24,28},{1,5},{5,9},{9,... | collective-permute-start | bytes 122888 | tf_op jit(solution)/shard_map/while/body/eval_jaxpr/ppermute | solution.py:10
  47.2 12.7 %collective-permute-start = (f32[1,32,320]{2,1,0:T(8,128)}, f32[1,32,320]{2,1,0:T(8,128)S(1)}, u32[]{:S(2)}, u32[]{:S(2)}) collective-permute-start(f32[1,32,320]{2,1,0:T(8,128)} %get-tuple-element.446), channel_id=1, source_target_pairs={{0,4},{4,8},{8,12},{12,16},{16,20},{20,24},{24,28},{1,5},{5,9},{9,... | collective-permute-start | bytes 122888 | tf_op jit(solution)/shard_map/while/body/eval_jaxpr/ppermute | solution.py:10
  60.5 5.6 %collective-permute-start = (f32[1,32,320]{2,1,0:T(8,128)}, f32[1,32,320]{2,1,0:T(8,128)S(1)}, u32[]{:S(2)}, u32[]{:S(2)}) collective-permute-start(f32[1,32,320]{2,1,0:T(8,128)} %get-tuple-element.446), channel_id=1, source_target_pairs={{0,4},{4,8},{8,12},{12,16},{16,20},{20,24},{24,28},{1,5},{5,9},{9,... | collective-permute-start | bytes 122888 | tf_op jit(solution)/shard_map/while/body/eval_jaxpr/ppermute | solution.py:10
  66.8 12.7 %collective-permute-start = (f32[1,32,320]{2,1,0:T(8,128)}, f32[1,32,320]{2,1,0:T(8,128)S(1)}, u32[]{:S(2)}, u32[]{:S(2)}) collective-permute-start(f32[1,32,320]{2,1,0:T(8,128)} %get-tuple-element.446), channel_id=1, source_target_pairs={{0,4},{4,8},{8,12},{12,16},{16,20},{20,24},{24,28},{1,5},{5,9},{9,... | collective-permute-start | bytes 122888 | tf_op jit(solution)/shard_map/while/body/eval_jaxpr/ppermute | solution.py:10
  80.1 5.6 %collective-permute-start = (f32[1,32,320]{2,1,0:T(8,128)}, f32[1,32,320]{2,1,0:T(8,128)S(1)}, u32[]{:S(2)}, u32[]{:S(2)}) collective-permute-start(f32[1,32,320]{2,1,0:T(8,128)} %get-tuple-element.446), channel_id=1, source_target_pairs={{0,4},{4,8},{8,12},{12,16},{16,20},{20,24},{24,28},{1,5},{5,9},{9,... | collective-permute-start | bytes 122888 | tf_op jit(solution)/shard_map/while/body/eval_jaxpr/ppermute | solution.py:10
  86.4 7.8 %collective-permute-start = (f32[1,32,320]{2,1,0:T(8,128)}, f32[1,32,320]{2,1,0:T(8,128)S(1)}, u32[]{:S(2)}, u32[]{:S(2)}) collective-permute-start(f32[1,32,320]{2,1,0:T(8,128)} %get-tuple-element.446), channel_id=1, source_target_pairs={{0,4},{4,8},{8,12},{12,16},{16,20},{20,24},{24,28},{1,5},{5,9},{9,... | collective-permute-start | bytes 122888 | tf_op jit(solution)/shard_map/while/body/eval_jaxpr/ppermute | solution.py:10
  94.8 6.1 %collective-permute-start = (f32[1,32,320]{2,1,0:T(8,128)}, f32[1,32,320]{2,1,0:T(8,128)S(1)}, u32[]{:S(2)}, u32[]{:S(2)}) collective-permute-start(f32[1,32,320]{2,1,0:T(8,128)} %get-tuple-element.446), channel_id=1, source_target_pairs={{0,4},{4,8},{8,12},{12,16},{16,20},{20,24},{24,28},{1,5},{5,9},{9,... | collective-permute-start | bytes 122888 | tf_op jit(solution)/shard_map/while/body/eval_jaxpr/ppermute | solution.py:10
  101.5 13.6 %collective-permute-start = (f32[1,32,320]{2,1,0:T(8,128)}, f32[1,32,320]{2,1,0:T(8,128)S(1)}, u32[]{:S(2)}, u32[]{:S(2)}) collective-permute-start(f32[1,32,320]{2,1,0:T(8,128)} %get-tuple-element.446), channel_id=1, source_target_pairs={{0,4},{4,8},{8,12},{12,16},{16,20},{20,24},{24,28},{1,5},{5,9},{9,... | collective-permute-start | bytes 122888 | tf_op jit(solution)/shard_map/while/body/eval_jaxpr/ppermute | solution.py:10
  115.2 172.6 %copy-start.3 = (s32[4,2]{0,1:T(2,128)S(1)}, s32[4,2]{0,1:T(2,128)}, u32[]{:S(2)}) copy-start(s32[4,2]{0,1:T(2,128)} %param.21) | copy-start | bytes 100
  115.2 173.0 %copy-start.2 = (s32[4,2]{0,1:T(2,128)S(1)}, s32[4,2]{0,1:T(2,128)}, u32[]{:S(2)}) copy-start(s32[4,2]{0,1:T(2,128)} %param.22) | copy-start | bytes 100
  115.9 6.4 %collective-permute-start.1 = (f32[1,32,320]{2,1,0:T(8,128)}, f32[1,32,320]{2,1,0:T(8,128)S(1)}, u32[]{:S(2)}, u32[]{:S(2)}) collective-permute-start(f32[1,32,320]{2,1,0:T(8,128)} %get-tuple-element.455), channel_id=1, source_target_pairs={{4,0},{8,4},{12,8},{16,12},{20,16},{24,20},{28,24},{5,1},{9,5},{13... | collective-permute-start | bytes 122888 | tf_op jit(solution)/shard_map/while/body/eval_jaxpr/ppermute | solution.py:10
  122.9 7.4 %collective-permute-start.1 = (f32[1,32,320]{2,1,0:T(8,128)}, f32[1,32,320]{2,1,0:T(8,128)S(1)}, u32[]{:S(2)}, u32[]{:S(2)}) collective-permute-start(f32[1,32,320]{2,1,0:T(8,128)} %get-tuple-element.455), channel_id=1, source_target_pairs={{4,0},{8,4},{12,8},{16,12},{20,16},{24,20},{28,24},{5,1},{9,5},{13... | collective-permute-start | bytes 122888 | tf_op jit(solution)/shard_map/while/body/eval_jaxpr/ppermute | solution.py:10
  131.0 6.4 %collective-permute-start.1 = (f32[1,32,320]{2,1,0:T(8,128)}, f32[1,32,320]{2,1,0:T(8,128)S(1)}, u32[]{:S(2)}, u32[]{:S(2)}) collective-permute-start(f32[1,32,320]{2,1,0:T(8,128)} %get-tuple-element.455), channel_id=1, source_target_pairs={{4,0},{8,4},{12,8},{16,12},{20,16},{24,20},{28,24},{5,1},{9,5},{13... | collective-permute-start | bytes 122888 | tf_op jit(solution)/shard_map/while/body/eval_jaxpr/ppermute | solution.py:10
  138.0 10.1 %collective-permute-start.1 = (f32[1,32,320]{2,1,0:T(8,128)}, f32[1,32,320]{2,1,0:T(8,128)S(1)}, u32[]{:S(2)}, u32[]{:S(2)}) collective-permute-start(f32[1,32,320]{2,1,0:T(8,128)} %get-tuple-element.455), channel_id=1, source_target_pairs={{4,0},{8,4},{12,8},{16,12},{20,16},{24,20},{28,24},{5,1},{9,5},{13... | collective-permute-start | bytes 122888 | tf_op jit(solution)/shard_map/while/body/eval_jaxpr/ppermute | solution.py:10
  148.7 6.5 %collective-permute-start.1 = (f32[1,32,320]{2,1,0:T(8,128)}, f32[1,32,320]{2,1,0:T(8,128)S(1)}, u32[]{:S(2)}, u32[]{:S(2)}) collective-permute-start(f32[1,32,320]{2,1,0:T(8,128)} %get-tuple-element.455), channel_id=1, source_target_pairs={{4,0},{8,4},{12,8},{16,12},{20,16},{24,20},{28,24},{5,1},{9,5},{13... | collective-permute-start | bytes 122888 | tf_op jit(solution)/shard_map/while/body/eval_jaxpr/ppermute | solution.py:10
  155.8 7.3 %collective-permute-start.1 = (f32[1,32,320]{2,1,0:T(8,128)}, f32[1,32,320]{2,1,0:T(8,128)S(1)}, u32[]{:S(2)}, u32[]{:S(2)}) collective-permute-start(f32[1,32,320]{2,1,0:T(8,128)} %get-tuple-element.455), channel_id=1, source_target_pairs={{4,0},{8,4},{12,8},{16,12},{20,16},{24,20},{28,24},{5,1},{9,5},{13... | collective-permute-start | bytes 122888 | tf_op jit(solution)/shard_map/while/body/eval_jaxpr/ppermute | solution.py:10
  163.8 53.5 %collective-permute-start.1 = (f32[1,32,320]{2,1,0:T(8,128)}, f32[1,32,320]{2,1,0:T(8,128)S(1)}, u32[]{:S(2)}, u32[]{:S(2)}) collective-permute-start(f32[1,32,320]{2,1,0:T(8,128)} %get-tuple-element.455), channel_id=1, source_target_pairs={{4,0},{8,4},{12,8},{16,12},{20,16},{24,20},{28,24},{5,1},{9,5},{13... | collective-permute-start | bytes 122888 | tf_op jit(solution)/shard_map/while/body/eval_jaxpr/ppermute | solution.py:10
  225.1 6.5 %collective-permute-start.1 = (f32[1,32,320]{2,1,0:T(8,128)}, f32[1,32,320]{2,1,0:T(8,128)S(1)}, u32[]{:S(2)}, u32[]{:S(2)}) collective-permute-start(f32[1,32,320]{2,1,0:T(8,128)} %get-tuple-element.455), channel_id=1, source_target_pairs={{4,0},{8,4},{12,8},{16,12},{20,16},{24,20},{28,24},{5,1},{9,5},{13... | collective-permute-start | bytes 122888 | tf_op jit(solution)/shard_map/while/body/eval_jaxpr/ppermute | solution.py:10
  239.6 6.5 %collective-permute-start.1 = (f32[1,32,320]{2,1,0:T(8,128)}, f32[1,32,320]{2,1,0:T(8,128)S(1)}, u32[]{:S(2)}, u32[]{:S(2)}) collective-permute-start(f32[1,32,320]{2,1,0:T(8,128)} %get-tuple-element.455), channel_id=1, source_target_pairs={{4,0},{8,4},{12,8},{16,12},{20,16},{24,20},{28,24},{5,1},{9,5},{13... | collective-permute-start | bytes 122888 | tf_op jit(solution)/shard_map/while/body/eval_jaxpr/ppermute | solution.py:10
  254.0 6.5 %collective-permute-start.1 = (f32[1,32,320]{2,1,0:T(8,128)}, f32[1,32,320]{2,1,0:T(8,128)S(1)}, u32[]{:S(2)}, u32[]{:S(2)}) collective-permute-start(f32[1,32,320]{2,1,0:T(8,128)} %get-tuple-element.455), channel_id=1, source_target_pairs={{4,0},{8,4},{12,8},{16,12},{20,16},{24,20},{28,24},{5,1},{9,5},{13... | collective-permute-start | bytes 122888 | tf_op jit(solution)/shard_map/while/body/eval_jaxpr/ppermute | solution.py:10
  268.4 3.3 %collective-permute-start.1 = (f32[1,32,320]{2,1,0:T(8,128)}, f32[1,32,320]{2,1,0:T(8,128)S(1)}, u32[]{:S(2)}, u32[]{:S(2)}) collective-permute-start(f32[1,32,320]{2,1,0:T(8,128)} %get-tuple-element.455), channel_id=1, source_target_pairs={{4,0},{8,4},{12,8},{16,12},{20,16},{24,20},{28,24},{5,1},{9,5},{13... | collective-permute-start | bytes 122888 | tf_op jit(solution)/shard_map/while/body/eval_jaxpr/ppermute | solution.py:10
  271.7 18.5 %copy-start.1 = (f32[4,2,32,320]{3,2,1,0:T(8,128)}, f32[4,2,32,320]{3,2,1,0:T(8,128)S(1)}, u32[]{:S(2)}) copy-start(f32[4,2,32,320]{3,2,1,0:T(8,128)S(1)} %get-tuple-element.330) | copy-start | bytes 983044
where the time goes:
time: 293 us; the launch traced here: 290 us
  waiting for transfers between devices  118 us (40%)
  starting transfers between devices  81.2 us (28%)
  matrix products  57.4 us (20%)
  blocking collectives  15.2 us (5%)
  local copies, waits for them, and re-layouts  10 us (3%)
  other arithmetic  6.46 us (2%)
    ppermute x22, waiting for transfers between devices, shifted(): lax.ppermute(value, axis, [(source, source + steps) for source in range(f...  118 us
    ppermute x22, starting transfers between devices, shifted(): lax.ppermute(value, axis, [(source, source + steps) for source in range(f...  81.2 us
    dot_general x32, matrix products, product(): jnp.einsum('lbc,lvc->lvb', blocks, vectors, precision=lax.Precision.HIGHEST)  56 us
    all_gather x1, blocking collectives, local(): segment = lax.all_gather(traces, 'theta', axis=0, tiled=True)  15.2 us
    another operation x18, local copies, waits for them, and re-layouts  8.79 us
    dynamic_update_slice x8, other arithmetic, working(): lax.dynamic_update_slice_in_dim(current, values, offset, 0)  6.45 us
  transfers between devices with their start and end apart: 22, of which 22 were waited for; matrix products, arithmetic and copies ran while one was open for 0% of the time, Pallas kernels for 0%

commit v1 on v0

v1 whole, which is shorter than its diff:
```python
import jax
import jax.numpy as jnp
from jax import lax
from jax.sharding import PartitionSpec as P

HIGH = lax.Precision.HIGH


def apply(blocks, vectors):
    return jnp.einsum("lbc,lvc->lvb", blocks, vectors, precision=HIGH)


def compose(left, right):
    return jnp.einsum("lbc,lcd->lbd", left, right, precision=HIGH)


def local(
    rhs_field,
    diag_inv,
    lower_block,
    upper_block,
    proj_table,
    intersection_list,
    proj_index,
    angle_step,
):
    lines, elems, vecs, size = rhs_field.shape
    devices = lax.axis_size("axial")
    chips = devices // 2
    half = lines // 2
    core = lax.axis_index("axial") % 2
    partner = [(d, d ^ 1) for d in range(devices)]

    def owned(value):
        mine = lax.dynamic_slice_in_dim(value, core * half, half, 0)
        other = lax.dynamic_slice_in_dim(value, (1 - core) * half, half, 0)
        got = lax.ppermute(other, "axial", partner)
        first = jnp.where(core == 0, mine, got)
        second = jnp.where(core == 0, got, mine)
        return jnp.concatenate([first, second], axis=1)

    def disowned(value):
        mine = lax.dynamic_slice_in_dim(value, core * elems, elems, 1)
        other = lax.dynamic_slice_in_dim(value, (1 - core) * elems, elems, 1)
        got = lax.ppermute(other, "axial", partner)
        first = jnp.where(core == 0, mine, got)
        second = jnp.where(core == 0, got, mine)
        return jnp.concatenate([first, second], axis=0)

    scaled = jnp.einsum("lebc,levc->levb", diag_inv, rhs_field, precision=HIGH)
    down = jnp.einsum("lebc,lecd->lebd", diag_inv, lower_block, precision=HIGH)
    up = jnp.einsum("lebc,lecd->lebd", diag_inv, upper_block, precision=HIGH)
    scaled, down = owned(scaled), owned(down)
    up = owned(up)
    count = 2 * elems

    parts = [scaled[:, 0]]
    maps = [-down[:, 0]]
    for e in range(1, count):
        parts.append(scaled[:, e] - apply(down[:, e], parts[-1]))
        maps.append(-compose(down[:, e], maps[-1]))

    incoming = jnp.zeros_like(parts[0])
    outgoing = parts[-1]
    for k in range(chips - 1):
        hop = [(2 * k + c, 2 * k + 2 + c) for c in range(2)]
        got = lax.ppermute(outgoing, "axial", hop)
        incoming = incoming + got
        outgoing = parts[-1] + apply(maps[-1], got)
    swept = [p + apply(m, incoming) for p, m in zip(parts, maps)]

    parts = [None] * count
    maps = [None] * count
    parts[-1] = swept[-1]
    maps[-1] = -up[:, -1]
    for e in reversed(range(count - 1)):
        parts[e] = swept[e] - apply(up[:, e], parts[e + 1])
        maps[e] = -compose(up[:, e], maps[e + 1])

    incoming = jnp.zeros_like(parts[0])
    outgoing = parts[0]
    for k in reversed(range(1, chips)):
        hop = [(2 * k + c, 2 * k - 2 + c) for c in range(2)]
        got = lax.ppermute(outgoing, "axial", hop)
        incoming = incoming + got
        outgoing = parts[0] + apply(maps[0], got)
    solved = jnp.stack([p + apply(m, incoming) for p, m in zip(parts, maps)], axis=1)
    solution = disowned(solved)

    face = proj_table.shape[1]
    traces = solution[:, -1, :, size - face :]
    groups = lax.axis_size("theta")
    here = lax.axis_index("theta")
    sources = (intersection_list + angle_step[0]) % (lines * groups)
    owner, place = sources // lines, sources % lines
    row_ids = jnp.arange(lines, dtype=jnp.int32)
    picked = 0.0
    for shift in range(groups):
        if shift:
            ring = [(t, (t + shift) % groups) for t in range(groups)]
            block = lax.ppermute(traces, "theta", ring)
        else:
            block = traces
        take = (owner == (here - shift) % groups)[:, :, None] & (
            place[:, :, None] == row_ids
        )
        picked = picked + jnp.einsum(
            "gkn,nvh->gkvh", take.astype(jnp.float32), block, precision=lax.Precision.HIGHEST
        )
    one_hot = jax.nn.one_hot(proj_index, proj_table.shape[0], dtype=jnp.float32)
    chosen = jnp.einsum("gkp,pfh->gkfh", one_hot, proj_table, precision=lax.Precision.HIGHEST)
    mortar = jnp.einsum("gkfh,gkvh->gvf", chosen, picked, precision=HIGH)
    return (solution, mortar.reshape(1, lines, vecs * face))


def solution(mesh):
    block = P("theta", "axial", None, None)
    return jax.shard_map(
        local,
        mesh=mesh,
        in_specs=(block, block, block, block, P(), P("theta", None), P("theta", None), P()),
        out_specs=(block, P("axial", "theta", None)),
        check_vma=False,
    )
```

time: 293 us -> 84.6 us (0.29)
  waiting for transfers between devices: 118 us -> 22.2 us
  starting transfers between devices: 81.2 us -> 15 us
  matrix products: 57.4 us -> 32.6 us
  blocking collectives: 15.2 us -> 0 us
    ppermute x22 -> x13, waiting for transfers between devices: 118 us -> 22.2 us  [the longest x6 17.2 us: local(): got = lax.ppermute(outgoing, 'axial', hop)]
    ppermute x22 -> x13, starting transfers between devices: 81.2 us -> 15 us  [the longest x6 9.23 us: local(): got = lax.ppermute(outgoing, 'axial', hop)]
    dot_general x34 -> x32, matrix products: 56.7 us -> 32 us  [the longest x18 10.1 us: apply(): return jnp.einsum('lbc,lvc->lvb', blocks, vectors, precision=HIGH)]
    all_gather x1 -> x0, blocking collectives: 15.2 us -> none  [local(): segment = lax.all_gather(traces, 'theta', axis=0, tiled=True)]
    another operation x18 -> x0, local copies, waits for them, and re-layouts: 8.79 us -> none
    dynamic_update_slice x8 -> x0, other arithmetic: 6.45 us -> none  [working(): lax.dynamic_update_slice_in_dim(current, values, offset, 0)]
    unnamed x11 -> x32, local copies, waits for them, and re-layouts: 0.29 us -> 4.94 us
    select_n x1 -> x6, other arithmetic: 0.01 us -> 4.37 us  [the longest x3 4.29 us: owned(): first = jnp.where(core == 0, mine, got)]
  transfers between devices with their start and end apart: 22 -> 13, of which waited for: 22 -> 4; matrix products, arithmetic and copies ran while one was open for 0% -> 26% of each run, Pallas kernels for 0% -> 0%
where the time goes in v1:
time: 84.6 us; the launch traced here: 84.3 us
  matrix products  32.6 us (39%)
  waiting for transfers between devices  22.2 us (26%)
  starting transfers between devices  15 us (18%)
  local copies, waits for them, and re-layouts  7.84 us (9%)
  other arithmetic  4.59 us (5%)
  between operations  1.98 us (2%)
    ppermute x6, waiting for transfers between devices, local(): got = lax.ppermute(outgoing, 'axial', hop)  17.2 us
    dot_general x18, matrix products, apply(): return jnp.einsum('lbc,lvc->lvb', blocks, vectors, precision=HIGH)  10.1 us
    ppermute x6, starting transfers between devices, local(): got = lax.ppermute(outgoing, 'axial', hop)  9.23 us
    dot_general x1, matrix products, local(): down = jnp.einsum('lebc,lecd->lebd', diag_inv, lower_block, precision=HIGH)  7.44 us
    dot_general x6, matrix products, compose(): return jnp.einsum('lbc,lcd->lbd', left, right, precision=HIGH)  6.69 us
    unnamed x32, local copies, waits for them, and re-layouts  4.94 us
    ppermute x3, starting transfers between devices, local(): block = lax.ppermute(traces, 'theta', ring)  4.68 us
    select_n x3, other arithmetic, owned(): first = jnp.where(core == 0, mine, got)  4.29 us
  transfers between devices with their start and end apart: 13, of which 4 were waited for; matrix products, arithmetic and copies ran while one was open for 26% of the time, Pallas kernels for 0%

profile of v1, /device:TPU:0, one launch (start us, length us, event | category | flops | bytes accessed | tf_op | source)
XLA Modules:
  0.0 84.3 jit_solution(16030340756300542176)
XLA Ops:
  0.7 7.4 %fusion.62 = f32[4,2,320,320]{3,2,1,0:T(8,128)S(1)} fusion(f32[4,2,320,320]{3,2,1,0:T(8,128)} %param.9, f32[4,2,320,320]{3,2,1,0:T(8,128)} %param.10), kind=kOutput, calls=%fused_computation.123 | convolution fusion | flops 1572864000 | bytes 9830400 | tf_op jit(solution)/shard_map/lebc,lecd->lebd/dot_general | solution.py:51
  8.1 1.5 %constant_dynamic-slice_fusion.2 = f32[2,2,320,320]{3,2,1,0:T(8,128)} fusion(f32[4,2,320,320]{3,2,1,0:T(8,128)S(1)} %fusion.62, s32[]{:T(128)S(6)} %select_n.93), kind=kLoop, calls=%fused_computation.104 | loop fusion | bytes 3276804 | tf_op jit(solution)/shard_map/dynamic_slice | solution.py:36
  9.6 1.5 %copy-done.6 = f32[4,2,320,320]{3,2,1,0:T(8,128)} copy-done((f32[4,2,320,320]{3,2,1,0:T(8,128)}, f32[4,2,320,320]{3,2,1,0:T(8,128)S(1)}, u32[]{:S(2)}) %copy-start.6) | copy-done | bytes 3276824
  11.6 0.8 copy-done.1
  12.4 1.9 %fusion.61 = f32[4,2,32,320]{3,2,1,0:T(8,128)S(1)} fusion(f32[4,2,32,320]{3,2,1,0:T(8,128)S(1)} %copy-done.12, f32[4,2,320,320]{3,2,1,0:T(8,128)S(1)} %copy-done.1), kind=kOutput, calls=%fused_computation.122 | convolution fusion | flops 157286400 | bytes 3932160 | tf_op jit(solution)/shard_map/lebc,levc->levb/dot_general | solution.py:50
  14.3 0.6 collective-permute-start
  14.9 4.2 %fusion.63 = f32[4,2,320,320]{3,2,1,0:T(8,128)S(1)} fusion(f32[4,2,320,320]{3,2,1,0:T(8,128)S(1)} %copy-done.1, f32[4,2,320,320]{3,2,1,0:T(8,128)S(1)} %copy-done.11), kind=kOutput, calls=%fused_computation.124 | convolution fusion | flops 1572864000 | bytes 9830400 | tf_op jit(solution)/shard_map/lebc,lecd->lebd/dot_general | solution.py:52
  19.3 1.7 %copy-done.4 = f32[4,2,320,320]{3,2,1,0:T(8,128)} copy-done((f32[4,2,320,320]{3,2,1,0:T(8,128)}, f32[4,2,320,320]{3,2,1,0:T(8,128)S(1)}, u32[]{:S(2)}) %copy-start.4) | copy-done | bytes 3276824
  21.8 2.5 %dynamic-slice_select_fusion.3 = (f32[2,2,320,320]{3,2,1,0:T(8,128)S(1)}, f32[2,2,320,320]{3,2,1,0:T(8,128)S(1)}) fusion(f32[2,2,320,320]{3,2,1,0:T(8,128)} %collective-permute-done.1, f32[4,2,320,320]{3,2,1,0:T(8,128)} %copy-done.6, s32[]{:T(128)S(6)} %select_n.92, pred[]{:T(512)S(6)} %eq.46), kind=kLoop, calls=%fused_computation.3 | loop fusion | flops 819200 | bytes 6553605 | tf_op jit(solution)/shard_map/jit(_where)/select_n | solution.py:38
  24.3 0.6 fusion.23
  24.9 0.6 fusion.10
  25.4 0.6 fusion.25
  26.0 5.0 %collective-permute-start.2 = (f32[2,32,320]{2,1,0:T(8,128)S(1)}, f32[2,32,320]{2,1,0:T(8,128)S(1)}, u32[]{:S(2)}, u32[]{:S(2)}) collective-permute-start(f32[2,32,320]{2,1,0:T(8,128)S(1)} %fusion.25), channel_id=1, source_target_pairs={{0,8},{4,12},{1,9},{5,13},{2,10},{6,14},{3,11},{7,15}} | collective-permute-start | bytes 245768 | tf_op jit(solution)/shard_map/ppermute | solution.py:67
  31.1 1.1 %convolution_negate_fusion.5 = f32[2,320,320]{2,1,0:T(8,128)S(1)} fusion(f32[2,2,320,320]{3,2,1,0:T(8,128)S(1)} %get-tuple-element.11), kind=kOutput, calls=%fused_computation.9 | convolution fusion | flops 393625600 | bytes 2457600 | tf_op jit(solution)/shard_map/lbc,lcd->lbd/dot_general | solution.py:14
  32.2 1.1 %convolution_negate_fusion.4 = f32[2,320,320]{2,1,0:T(8,128)S(1)} fusion(f32[2,320,320]{2,1,0:T(8,128)S(1)} %convolution_negate_fusion.5, f32[2,2,320,320]{3,2,1,0:T(8,128)S(1)} %get-tuple-element.12), kind=kOutput, calls=%fused_computation.8 | convolution fusion | flops 393420800 | bytes 2785280 | tf_op jit(solution)/shard_map/lbc,lcd->lbd/dot_general | solution.py:14
  33.4 1.8 %dynamic-slice_select_fusion = (f32[2,2,320,320]{3,2,1,0:T(8,128)S(1)}, f32[2,2,320,320]{3,2,1,0:T(8,128)S(1)}) fusion(f32[2,2,320,320]{3,2,1,0:T(8,128)} %collective-permute-done.5, f32[4,2,320,320]{3,2,1,0:T(8,128)S(1)} %copy-done.5, s32[]{:T(128)S(6)} %select_n.92, pred[]{:T(512)S(6)} %eq.46), kind=kLoop, calls=%fused_computation | loop fusion | flops 819200 | bytes 6553605 | tf_op jit(solution)/shard_map/jit(_where)/select_n | solution.py:38
  35.2 1.1 %convolution_negate_fusion.3 = f32[2,320,320]{2,1,0:T(8,128)S(1)} fusion(f32[2,320,320]{2,1,0:T(8,128)S(1)} %convolution_negate_fusion.4, f32[2,2,320,320]{3,2,1,0:T(8,128)S(1)} %get-tuple-element.12), kind=kOutput, calls=%fused_computation.7 | convolution fusion | flops 393420800 | bytes 2785280 | tf_op jit(solution)/shard_map/lbc,lcd->lbd/dot_general | solution.py:14
  36.3 0.6 convolution_add_fusion.11
  36.9 0.7 collective-permute-start.3
  37.6 1.1 %convolution_negate_fusion.2 = f32[2,320,320]{2,1,0:T(8,128)S(1)} fusion(f32[2,2,320,320]{3,2,1,0:T(8,128)S(1)} %get-tuple-element.10), kind=kOutput, calls=%fused_computation.6 | convolution fusion | flops 393625600 | bytes 2457600 | tf_op jit(solution)/shard_map/lbc,lcd->lbd/dot_general | solution.py:14
  38.7 0.6 convolution_add_fusion.10
  39.3 0.7 collective-permute-start.4
  39.9 1.1 %convolution_negate_fusion.1 = f32[2,320,320]{2,1,0:T(8,128)S(1)} fusion(f32[2,320,320]{2,1,0:T(8,128)S(1)} %convolution_negate_fusion.2, f32[2,2,320,320]{3,2,1,0:T(8,128)S(1)} %get-tuple-element.9), kind=kOutput, calls=%fused_computation.5 | convolution fusion | flops 393420800 | bytes 2785280 | tf_op jit(solution)/shard_map/lbc,lcd->lbd/dot_general | solution.py:14
  41.1 0.6 convolution_add_fusion.6
  41.7 0.6 fusion.12
  42.2 0.6 fusion.4
  42.8 0.6 fusion.13
  43.4 0.6 fusion.5
  44.0 0.6 fusion.14
  44.5 0.6 fusion.6
  45.1 0.7 collective-permute-start.6
  45.8 1.1 %convolution_negate_fusion = f32[2,320,320]{2,1,0:T(8,128)S(1)} fusion(f32[2,320,320]{2,1,0:T(8,128)S(1)} %convolution_negate_fusion.1, f32[2,2,320,320]{3,2,1,0:T(8,128)S(1)} %get-tuple-element.9), kind=kOutput, calls=%fused_computation.4 | convolution fusion | flops 393420800 | bytes 2785280 | tf_op jit(solution)/shard_map/lbc,lcd->lbd/dot_general | solution.py:14
  46.9 0.6 convolution_add_fusion.5
  47.5 0.7 collective-permute-start.7
  48.2 0.6 convolution_add_fusion.4
  48.8 1.5 %collective-permute-start.8 = (f32[2,32,320]{2,1,0:T(8,128)S(1)}, f32[2,32,320]{2,1,0:T(8,128)S(1)}, u32[]{:S(2)}, u32[]{:S(2)}) collective-permute-start(f32[2,32,320]{2,1,0:T(8,128)S(1)} %convolution_add_fusion.4), channel_id=1, source_target_pairs={{8,0},{12,4},{9,1},{13,5},{10,2},{14,6},{11,3},{15,7}} | collective-permute-start | bytes 245768 | tf_op jit(solution)/shard_map/ppermute | solution.py:84
  50.9 17.2 %collective-permute-done.8 = f32[2,32,320]{2,1,0:T(8,128)S(1)} collective-permute-done((f32[2,32,320]{2,1,0:T(8,128)S(1)}, f32[2,32,320]{2,1,0:T(8,128)S(1)}, u32[]{:S(2)}, u32[]{:S(2)}) %collective-permute-start.8) | collective-permute-done | bytes 81952 | tf_op jit(solution)/shard_map/ppermute | solution.py:84
  68.1 0.6 fusion
  68.7 0.6 fusion.1
  69.3 0.6 fusion.2
  69.9 0.6 fusion.3
  70.6 0.7 fusion.19
  71.3 0.7 collective-permute-done.9
  72.2 3.7 %collective-permute-start.12 = (f32[4,32,80]{2,1,0:T(8,128)S(1)}, f32[4,32,80]{2,1,0:T(8,128)S(1)}, u32[]{:S(2)}, u32[]{:S(2)}) collective-permute-start(f32[4,32,80]{2,1,0:T(8,128)S(1)} %get-tuple-element.16), channel_id=1, source_target_pairs={{0,3},{1,0},{2,1},{3,2},{4,7},{5,4},{6,5},{7,6},{8,11},{9,8},{10,9... | collective-permute-start | bytes 122888 | tf_op jit(solution)/shard_map/ppermute | solution.py:101
  75.9 1.0 %collective-permute-start.10 = (f32[4,32,80]{2,1,0:T(8,128)S(1)}, f32[4,32,80]{2,1,0:T(8,128)S(1)}, u32[]{:S(2)}, u32[]{:S(2)}) collective-permute-start(f32[4,32,80]{2,1,0:T(8,128)S(1)} %get-tuple-element.16), channel_id=1, source_target_pairs={{0,1},{1,2},{2,3},{3,0},{4,5},{5,6},{6,7},{7,4},{8,9},{9,10},{10,1... | collective-permute-start | bytes 122888 | tf_op jit(solution)/shard_map/ppermute | solution.py:101
  77.2 0.8 copy.21
  78.7 3.9 %collective-permute-done.11 = f32[4,32,80]{2,1,0:T(8,128)S(1)} collective-permute-done((f32[4,32,80]{2,1,0:T(8,128)S(1)}, f32[4,32,80]{2,1,0:T(8,128)S(1)}, u32[]{:S(2)}, u32[]{:S(2)}) %collective-permute-start.11) | collective-permute-done | bytes 40992 | tf_op jit(solution)/shard_map/ppermute | solution.py:101
  83.6 0.7 reshape.15
  (66 shorter events, 3.7 us)
Async XLA Ops:
  0.6 70.0 %copy-start = (f32[16,80,80]{2,1,0:T(8,128)S(1)}, f32[16,80,80]{2,1,0:T(8,128)}, u32[]{:S(2)}) copy-start(f32[16,80,80]{2,1,0:T(8,128)} %param.12) | copy-start | bytes 1228804
  0.7 11.0 %copy-start.12 = (f32[4,2,32,320]{3,2,1,0:T(8,128)S(1)}, f32[4,2,32,320]{3,2,1,0:T(8,128)}, u32[]{:S(2)}) copy-start(f32[4,2,32,320]{3,2,1,0:T(8,128)} %param.8) | copy-start | bytes 983044
  8.1 3.0 %copy-start.6 = (f32[4,2,320,320]{3,2,1,0:T(8,128)}, f32[4,2,320,320]{3,2,1,0:T(8,128)S(1)}, u32[]{:S(2)}) copy-start(f32[4,2,320,320]{3,2,1,0:T(8,128)S(1)} %fusion.62) | copy-start | bytes 9830404
  8.1 4.2 %copy-start.1 = (f32[4,2,320,320]{3,2,1,0:T(8,128)S(1)}, f32[4,2,320,320]{3,2,1,0:T(8,128)}, u32[]{:S(2)}) copy-start(f32[4,2,320,320]{3,2,1,0:T(8,128)} %param.9) | copy-start | bytes 9830404
  11.1 3.8 %copy-start.11 = (f32[4,2,320,320]{3,2,1,0:T(8,128)S(1)}, f32[4,2,320,320]{3,2,1,0:T(8,128)}, u32[]{:S(2)}) copy-start(f32[4,2,320,320]{3,2,1,0:T(8,128)} %param.11) | copy-start | bytes 9830404
  11.1 10.7 %collective-permute-start.1 = (f32[2,2,320,320]{3,2,1,0:T(8,128)}, f32[2,2,320,320]{3,2,1,0:T(8,128)}, u32[]{:S(2)}, u32[]{:S(2)}) collective-permute-start(f32[2,2,320,320]{3,2,1,0:T(8,128)} %constant_dynamic-slice_fusion.2), channel_id=1, source_target_pairs={{0,4},{4,0},{8,12},{12,8},{16,20},{20,16},{24,28},{28,24},{1,5},{5... | collective-permute-start | bytes 4915208 | tf_op jit(solution)/shard_map/ppermute | solution.py:37
  14.3 7.4 %collective-permute-start = (f32[2,2,32,320]{3,2,1,0:T(8,128)S(1)}, f32[2,2,32,320]{3,2,1,0:T(8,128)S(1)}, u32[]{:S(2)}, u32[]{:S(2)}) collective-permute-start(f32[2,2,32,320]{3,2,1,0:T(8,128)S(1)} %constant_dynamic-slice_fusion.3), channel_id=1, source_target_pairs={{0,4},{4,0},{8,12},{12,8},{16,20},{20,16},{24,28},{28,24},{1,5},{5... | collective-permute-start | bytes 491528 | tf_op jit(solution)/shard_map/ppermute | solution.py:37
  19.1 1.9 %copy-start.4 = (f32[4,2,320,320]{3,2,1,0:T(8,128)}, f32[4,2,320,320]{3,2,1,0:T(8,128)S(1)}, u32[]{:S(2)}) copy-start(f32[4,2,320,320]{3,2,1,0:T(8,128)S(1)} %fusion.63) | copy-start | bytes 9830404
  19.1 2.6 %copy-start.14 = (s32[4,2]{0,1:T(2,128)S(1)}, s32[4,2]{0,1:T(2,128)}, u32[]{:S(2)}) copy-start(s32[4,2]{0,1:T(2,128)} %param.13) | copy-start | bytes 100
  21.0 12.4 %collective-permute-start.5 = (f32[2,2,320,320]{3,2,1,0:T(8,128)S(1)}, f32[2,2,320,320]{3,2,1,0:T(8,128)}, u32[]{:S(2)}, u32[]{:S(2)}) collective-permute-start(f32[2,2,320,320]{3,2,1,0:T(8,128)S(1)} %constant_dynamic-slice_fusion.1), channel_id=1, source_target_pairs={{0,4},{4,0},{8,12},{12,8},{16,20},{20,16},{24,28},{28,24},{1,5},{5... | collective-permute-start | bytes 4915208 | tf_op jit(solution)/shard_map/ppermute | solution.py:37
  26.0 10.3 %collective-permute-start.2 = (f32[2,32,320]{2,1,0:T(8,128)S(1)}, f32[2,32,320]{2,1,0:T(8,128)S(1)}, u32[]{:S(2)}, u32[]{:S(2)}) collective-permute-start(f32[2,32,320]{2,1,0:T(8,128)S(1)} %fusion.25), channel_id=1, source_target_pairs={{0,8},{4,12},{1,9},{5,13},{2,10},{6,14},{3,11},{7,15}} | collective-permute-start | bytes 245768 | tf_op jit(solution)/shard_map/ppermute | solution.py:67
  31.1 2.3 %copy-start.5 = (f32[4,2,320,320]{3,2,1,0:T(8,128)S(1)}, f32[4,2,320,320]{3,2,1,0:T(8,128)}, u32[]{:S(2)}) copy-start(f32[4,2,320,320]{3,2,1,0:T(8,128)} %copy-done.4) | copy-start | bytes 9830404
  36.9 1.8 %collective-permute-start.3 = (f32[2,32,320]{2,1,0:T(8,128)S(1)}, f32[2,32,320]{2,1,0:T(8,128)S(1)}, u32[]{:S(2)}, u32[]{:S(2)}) collective-permute-start(f32[2,32,320]{2,1,0:T(8,128)S(1)} %convolution_add_fusion.11), channel_id=1, source_target_pairs={{8,16},{12,20},{9,17},{13,21},{10,18},{14,22},{11,19},{15,23}} | collective-permute-start | bytes 245768 | tf_op jit(solution)/shard_map/ppermute | solution.py:67
  38.7 2.4 %copy-start.7 = (f32[2,320,320]{2,1,0:T(8,128)}, f32[2,320,320]{2,1,0:T(8,128)S(1)}, u32[]{:S(2)}) copy-start(f32[2,320,320]{2,1,0:T(8,128)S(1)} %convolution_negate_fusion.2) | copy-start | bytes 2457604
  39.3 1.8 %collective-permute-start.4 = (f32[2,32,320]{2,1,0:T(8,128)S(1)}, f32[2,32,320]{2,1,0:T(8,128)S(1)}, u32[]{:S(2)}, u32[]{:S(2)}) collective-permute-start(f32[2,32,320]{2,1,0:T(8,128)S(1)} %convolution_add_fusion.10), channel_id=1, source_target_pairs={{16,24},{20,28},{17,25},{21,29},{18,26},{22,30},{19,27},{23,31}} | collective-permute-start | bytes 245768 | tf_op jit(solution)/shard_map/ppermute | solution.py:67
  41.0 4.7 %copy-start.9 = (f32[2,320,320]{2,1,0:T(8,128)}, f32[2,320,320]{2,1,0:T(8,128)S(1)}, u32[]{:S(2)}) copy-start(f32[2,320,320]{2,1,0:T(8,128)S(1)} %convolution_negate_fusion.1) | copy-start | bytes 2457604
  45.1 1.8 %collective-permute-start.6 = (f32[2,32,320]{2,1,0:T(8,128)S(1)}, f32[2,32,320]{2,1,0:T(8,128)S(1)}, u32[]{:S(2)}, u32[]{:S(2)}) collective-permute-start(f32[2,32,320]{2,1,0:T(8,128)S(1)} %fusion.6), channel_id=1, source_target_pairs={{24,16},{28,20},{25,17},{29,21},{26,18},{30,22},{27,19},{31,23}} | collective-permute-start | bytes 245768 | tf_op jit(solution)/shard_map/ppermute | solution.py:84
  46.9 1.3 %copy-start.2 = (f32[2,320,320]{2,1,0:T(8,128)}, f32[2,320,320]{2,1,0:T(8,128)S(1)}, u32[]{:S(2)}) copy-start(f32[2,320,320]{2,1,0:T(8,128)S(1)} %convolution_negate_fusion) | copy-start | bytes 2457604
  46.9 3.4 %copy-start.13 = (s32[4,2]{0,1:T(2,128)S(1)}, s32[4,2]{0,1:T(2,128)}, u32[]{:S(2)}) copy-start(s32[4,2]{0,1:T(2,128)} %param.14) | copy-start | bytes 100
  47.5 0.7 collective-permute-start.7
  48.8 19.4 %collective-permute-start.8 = (f32[2,32,320]{2,1,0:T(8,128)S(1)}, f32[2,32,320]{2,1,0:T(8,128)S(1)}, u32[]{:S(2)}, u32[]{:S(2)}) collective-permute-start(f32[2,32,320]{2,1,0:T(8,128)S(1)} %convolution_add_fusion.4), channel_id=1, source_target_pairs={{8,0},{12,4},{9,1},{13,5},{10,2},{14,6},{11,3},{15,7}} | collective-permute-start | bytes 245768 | tf_op jit(solution)/shard_map/ppermute | solution.py:84
  50.9 17.8 %copy-start.8 = (f32[2,320,320]{2,1,0:T(8,128)S(1)}, f32[2,320,320]{2,1,0:T(8,128)}, u32[]{:S(2)}) copy-start(f32[2,320,320]{2,1,0:T(8,128)} %copy-done.7) | copy-start | bytes 2457604
  50.9 18.4 %copy-start.10 = (f32[2,320,320]{2,1,0:T(8,128)S(1)}, f32[2,320,320]{2,1,0:T(8,128)}, u32[]{:S(2)}) copy-start(f32[2,320,320]{2,1,0:T(8,128)} %copy-done.9) | copy-start | bytes 2457604
  68.1 1.8 %copy-start.3 = (f32[2,320,320]{2,1,0:T(8,128)S(1)}, f32[2,320,320]{2,1,0:T(8,128)}, u32[]{:S(2)}) copy-start(f32[2,320,320]{2,1,0:T(8,128)} %copy-done.2) | copy-start | bytes 2457604
  70.5 1.5 %collective-permute-start.9 = (f32[2,2,32,320]{3,2,0,1:T(8,128)S(1)}, f32[2,2,32,320]{3,2,0,1:T(8,128)S(1)}, u32[]{:S(2)}, u32[]{:S(2)}) collective-permute-start(f32[2,2,32,320]{3,2,0,1:T(8,128)S(1)} %constant_dynamic-slice_fusion), channel_id=1, source_target_pairs={{0,4},{4,0},{8,12},{12,8},{16,20},{20,16},{24,28},{28,24},{1,5},{5... | collective-permute-start | bytes 491528 | tf_op jit(solution)/shard_map/ppermute | solution.py:45
  72.2 6.2 %collective-permute-start.12 = (f32[4,32,80]{2,1,0:T(8,128)S(1)}, f32[4,32,80]{2,1,0:T(8,128)S(1)}, u32[]{:S(2)}, u32[]{:S(2)}) collective-permute-start(f32[4,32,80]{2,1,0:T(8,128)S(1)} %get-tuple-element.16), channel_id=1, source_target_pairs={{0,3},{1,0},{2,1},{3,2},{4,7},{5,4},{6,5},{7,6},{8,11},{9,8},{10,9... | collective-permute-start | bytes 122888 | tf_op jit(solution)/shard_map/ppermute | solution.py:101
  75.9 6.8 %collective-permute-start.11 = (f32[4,32,80]{2,1,0:T(8,128)S(1)}, f32[4,32,80]{2,1,0:T(8,128)S(1)}, u32[]{:S(2)}, u32[]{:S(2)}) collective-permute-start(f32[4,32,80]{2,1,0:T(8,128)S(1)} %get-tuple-element.16), channel_id=1, source_target_pairs={{0,2},{1,3},{2,0},{3,1},{4,6},{5,7},{6,4},{7,5},{8,10},{9,11},{10,... | collective-permute-start | bytes 122888 | tf_op jit(solution)/shard_map/ppermute | solution.py:101
  75.9 7.1 %collective-permute-start.10 = (f32[4,32,80]{2,1,0:T(8,128)S(1)}, f32[4,32,80]{2,1,0:T(8,128)S(1)}, u32[]{:S(2)}, u32[]{:S(2)}) collective-permute-start(f32[4,32,80]{2,1,0:T(8,128)S(1)} %get-tuple-element.16), channel_id=1, source_target_pairs={{0,1},{1,2},{2,3},{3,0},{4,5},{5,6},{6,7},{7,4},{8,9},{9,10},{10,1... | collective-permute-start | bytes 122888 | tf_op jit(solution)/shard_map/ppermute | solution.py:101
